TPU v7x, 512 devices: a whole 4x8x8 slice. The times are simulated.
512 devices in a mesh: tok: 16 (over z, core), voc: 32 (over y, x).
Axes of the slice: x: 4, y: 8, z: 8, core: 2. Of those that a mesh axis runs over, the one named last changes fastest.
Arguments:
- hidden: bfloat16 [256, 2304], P('tok', 'voc'), may hold values from -18 to 18
- head: bfloat16 [2304, 131072], P(None, ('tok', 'voc')), as said below
- targets: int32 [256], replicated, may hold values from 0 to 131071
- probe_hidden: bfloat16 [256, 2304], P('tok', 'voc'), may hold values from -6 to 6
- probe_head: bfloat16 [2304, 131072], P(None, ('tok', 'voc')), may hold values from -0.5 to 0.5
Outputs:
- head_out: float32 [2304, 131072], P(None, ('tok', 'voc'))
- hidden_out: float32 [256, 2304], P('tok', 'voc')
Inputs may be any that keep to these rules, and one draw needn't show every extreme that they name: `head`: entries lie within 66 / sqrt(2304) in magnitude.
All inputs are finite; a program needn't handle non-finite values.
Results may differ from a plain program's by a relative error of at most 0.0075.
Values may be sent and summed in bfloat16 or wider, within the bound.
A program may use at most 64 MiB of HBM per device.

v0:
```python
import jax
import jax.numpy as jnp
from jax import lax
from jax.sharding import PartitionSpec as P

softcap_value = 30.0
zloss_weight = 0.0001


def local(hidden, head, targets, probe_hidden, probe_head):
    voc_count = lax.axis_size("voc")
    vocab_width = head.shape[1]
    stacked = jnp.stack([hidden, probe_hidden])
    features = lax.all_gather(stacked, "voc", axis=2, tiled=True)
    gathered = lax.all_gather(features, "tok", axis=1, tiled=True)
    row_hidden = gathered[0]
    row_probe = gathered[1]
    logits = jnp.dot(row_hidden, head, preferred_element_type=jnp.float32)
    tangent = jnp.dot(row_probe, head, preferred_element_type=jnp.float32) + jnp.dot(
        row_hidden, probe_head, preferred_element_type=jnp.float32
    )
    capped = jnp.tanh(logits / softcap_value)
    cap_slope = 1.0 - capped * capped
    exponent = jnp.exp(softcap_value * capped)
    cap_tangent = cap_slope * tangent
    stats = lax.psum(
        jnp.stack([jnp.sum(exponent, axis=1), jnp.sum(exponent * cap_tangent, axis=1)]),
        ("tok", "voc"),
    )
    row_total = stats[0]
    probability = exponent / row_total[:, None]
    mean_tangent = stats[1] / row_total
    factor = 1.0 + 2.0 * zloss_weight * jnp.log(row_total)
    offset = (lax.axis_index("tok") * voc_count + lax.axis_index("voc")) * vocab_width
    columns = offset + lax.iota(jnp.int32, vocab_width)
    onehot = (targets[:, None] == columns[None, :]).astype(jnp.float32)
    grad_cap = factor[:, None] * probability - onehot
    grad_tan = probability * (
        factor[:, None] * (cap_tangent - mean_tangent[:, None])
        + 2.0 * zloss_weight * mean_tangent[:, None]
    )
    slope_tan = -2.0 / softcap_value * capped * cap_slope * tangent
    dlogit = (grad_cap * cap_slope).astype(jnp.bfloat16)
    dlogit_tan = (grad_tan * cap_slope + grad_cap * slope_tan).astype(jnp.bfloat16)
    head_out = jnp.einsum(
        "krd,krv->dv", gathered, jnp.stack([dlogit_tan, dlogit]), preferred_element_type=jnp.float32
    )
    probe_part = lax.dot_general(
        dlogit, probe_head, (((1,), (1,)), ((), ())), preferred_element_type=jnp.float32
    )
    head_part = lax.dot_general(
        dlogit_tan, head, (((1,), (1,)), ((), ())), preferred_element_type=jnp.float32
    )
    summed = lax.psum_scatter(probe_part + head_part, "tok", scatter_dimension=0, tiled=True)
    hidden_out = lax.psum_scatter(summed, "voc", scatter_dimension=1, tiled=True)
    return (head_out, hidden_out)


def solution(mesh):
    return jax.shard_map(
        local,
        mesh=mesh,
        in_specs=(
            P("tok", "voc"),
            P(None, ("tok", "voc")),
            P(),
            P("tok", "voc"),
            P(None, ("tok", "voc")),
        ),
        out_specs=(P(None, ("tok", "voc")), P("tok", "voc")),
        check_vma=False,
    )
```

profile of v0, /device:TPU:2, one launch (start us, length us, event | category | flops | bytes accessed | tf_op | source)
XLA Modules:
  0.0 435.7 jit_solution(9446589212632024018)
XLA Ops:
  7.2 0.0 copy-start
  7.2 0.0 all-gather.2.cloned.1.call-start
  7.2 0.8 pad_maximum_fusion
  8.0 0.1 copy.12
  8.1 52.7 %all_gather.6 = bf16[2,16,2304]{1,0,2:T(2,128)(2,1)S(1)} all-gather(bf16[2,16,72]{1,0,2:T(2,128)(2,1)S(1)} %copy.12), channel_id=1, replica_groups=mesh['tok'=16,'voc'=32] {'voc'}, dimensions={2}, use_global_device_ids=true | all-gather | bytes 152064 | tf_op jit(solution)/shard_map/all_gather | solution.py:14
  60.8 2.2 copy.13
  63.0 0.0 all-gather.2.cloned.1.call-update
  63.0 0.0 reduce-scatter.3.cloned.1.call-start
  63.1 43.3 %all-gather.2.cloned.1.call-done = bf16[2,256,2304]{2,1,0:T(8,128)(2,1)} async-done(((bf16[2,16,2304]{2,1,0:T(8,128)(2,1)}), bf16[2,256,2304]{2,1,0:T(8,128)(2,1)}) %all-gather.2.cloned.1.call-update) | async-done | bytes 2359312 | tf_op jit(solution)/shard_map/all_gather | solution.py:15
  106.4 2.4 fusion.3
  108.7 0.6 fusion.1
  109.4 1.3 fusion.9
  110.7 96.8 %psum.7 = f32[2,256]{1,0:T(2,128)S(1)} all-reduce(f32[2,256]{1,0:T(2,128)S(1)} %pad_maximum_fusion.1), channel_id=1, replica_groups=mesh['tok'=16,'voc'=32] {'tok','voc'}, use_global_device_ids=true, to_apply=%region_2.0 | all-reduce | flops 512 | bytes 4096 | tf_op jit(solution)/shard_map/psum | solution.py:26
  207.5 1.2 add_convert_fusion
  208.8 1.9 fusion.12
  210.7 2.0 convolution_add_fusion
  212.6 0.0 reduce-scatter.3.cloned.1.call-update
  212.7 0.0 all-reduce.3.cloned.1.call-start
  212.7 1.3 dynamic-slice
  214.6 57.4 %reduce-scatter.3.cloned.1.call-done = f32[16,2304]{1,0:T(8,128)} async-done(((f32[256,2304]{1,0:T(8,128)}), f32[16,2304]{1,0:T(8,128)}) %reduce-scatter.3.cloned.1.call-update) | async-done | bytes 147472 | tf_op jit(solution)/shard_map/reduce_scatter | solution.py:54
  272.0 0.0 all-reduce.3.cloned.1.call-update
  272.1 3.2 convolution_bitcast_fusion
  275.3 152.5 %all-reduce.3.cloned.1.call-done = f32[16,2304]{1,0:T(8,128)} async-done(((f32[16,2304]{1,0:T(8,128)}), f32[16,2304]{1,0:T(8,128)}) %all-reduce.3.cloned.1.call-update) | async-done | bytes 147472
  427.8 1.4 constant_dynamic-slice_fusion
  (15 shorter events, 0.1 us)
Async XLA Ops:
  7.2 101.6 %copy-start = (bf16[2304,256]{1,0:T(8,128)(2,1)S(1)}, bf16[2304,256]{1,0:T(8,128)(2,1)}, u32[]{:S(2)}) copy-start(bf16[2304,256]{1,0:T(8,128)(2,1)} %param.6) | copy-start | bytes 3538948
  7.2 99.2 %all-gather.2.cloned.1.call-start = ((), (), s32[]{:S(2)}) async-start(), calls=%async_computation.1 | async-start | bytes 2506752 | tf_op jit(solution)/shard_map/all_gather | solution.py:15
  63.0 209.0 %reduce-scatter.3.cloned.1.call-start = ((), (), s32[]{:S(2)}) async-start(), calls=%async_computation.2 | async-start | bytes 2506752 | tf_op jit(solution)/shard_map/reduce_scatter | solution.py:54
  106.4 2.4 copy-start.1
  109.3 1.3 copy-start.4
  109.4 98.1 %copy-start.5 = (s32[256]{0:T(256)S(1)}, s32[256]{0:T(256)}, u32[]{:S(2)}) copy-start(s32[256]{0:T(256)} %param.7) | copy-start | bytes 3076
  208.7 1.9 copy-start.3
  208.8 1.9 copy-start.2
  212.7 215.1 %all-reduce.3.cloned.1.call-start = ((), (), s32[]{:S(2)}) async-start(), calls=%async_computation.3 | async-start | bytes 294912
Sparse Core Ops, SparseCore 0:
  63.1 43.1 all-gather.1
  212.8 59.2 reduce-scatter.2
  275.5 152.2 all-reduce.2
where the time goes:
time: 436 us
  waiting for transfers between devices  253 us (58%)
  blocking collectives  149 us (34%)
  between operations  14.5 us (3%)
  matrix products  11.3 us (3%)
  local copies, waits for them, and re-layouts  5.01 us (1%)
    unnamed x4, waiting for transfers between devices  153 us
    psum x1, blocking collectives, local(): lax.psum(jnp.stack([jnp.sum(exponent, axis=1), jnp.sum(exponent * cap_tan...  96.8 us
    reduce_scatter x1, waiting for transfers between devices, local(): lax.psum_scatter(probe_part + head_part, 'tok', scatter_dimension=0, tile...  57.4 us
    all_gather x1, blocking collectives, local(): features = lax.all_gather(stacked, 'voc', axis=2, tiled=True)  52.7 us
    all_gather x1, waiting for transfers between devices, local(): gathered = lax.all_gather(features, 'tok', axis=1, tiled=True)  43.3 us
  transfers between devices with their start and end apart: 3, of which 3 were waited for; matrix products, arithmetic and copies ran while one was open for 1% of the time, Pallas kernels for 0%

commit v1 on v0

--- a/solution.py
+++ b/solution.py
@@ -7,11 +7,16 @@
 zloss_weight = 0.0001
 
 
+def all_by_exchange(x, name, dim):
+    sent = jnp.stack([x] * lax.axis_size(name))
+    return jnp.concatenate(lax.all_to_all(sent, name, 0, 0), axis=dim)
+
+
 def local(hidden, head, targets, probe_hidden, probe_head):
     voc_count = lax.axis_size("voc")
     vocab_width = head.shape[1]
     stacked = jnp.stack([hidden, probe_hidden])
-    features = lax.all_gather(stacked, "voc", axis=2, tiled=True)
+    features = all_by_exchange(stacked, "voc", 2)
     gathered = lax.all_gather(features, "tok", axis=1, tiled=True)
     row_hidden = gathered[0]
     row_probe = gathered[1]

time: 436 us -> 403 us (0.924)
  blocking collectives: 149 us -> 118 us
    all_gather x1 -> x0, blocking collectives: 52.7 us -> none  [local(): features = lax.all_gather(stacked, 'voc', axis=2, tiled=True)]
    all_to_all x0 -> x1, blocking collectives: none -> 21.3 us  [all_by_exchange(): return jnp.concatenate(lax.all_to_all(sent, name, 0, 0), axis=dim)]
where the time goes in v1:
time: 403 us
  waiting for transfers between devices  253 us (63%)
  blocking collectives  118 us (29%)
  between operations  14.5 us (4%)
  matrix products  11.3 us (3%)
    unnamed x4, waiting for transfers between devices  153 us
    psum x1, blocking collectives, local(): lax.psum(jnp.stack([jnp.sum(exponent, axis=1), jnp.sum(exponent * cap_tan...  96.8 us
    reduce_scatter x1, waiting for transfers between devices, local(): lax.psum_scatter(probe_part + head_part, 'tok', scatter_dimension=0, tile...  57.4 us
    all_gather x1, waiting for transfers between devices, local(): gathered = lax.all_gather(features, 'tok', axis=1, tiled=True)  43.2 us
    all_to_all x1, blocking collectives, all_by_exchange(): return jnp.concatenate(lax.all_to_all(sent, name, 0, 0), axis=dim)  21.3 us
  transfers between devices with their start and end apart: 3, of which 3 were waited for; matrix products, arithmetic and copies ran while one was open for 1% of the time, Pallas kernels for 0%

profile of v1, /device:TPU:2, one launch (start us, length us, event | category | flops | bytes accessed | tf_op | source)
XLA Modules:
  0.0 403.1 jit_solution(1497613488664171501)
XLA Ops:
  7.2 0.0 copy-start
  7.2 0.0 all-gather.2.cloned.1.call-start
  7.2 0.8 pad_maximum_fusion
  8.1 21.3 %all_to_all.5 = bf16[32,2,16,72]{3,2,1,0:T(8,128)(2,1)S(1)} all-to-all(bf16[32,2,16,72]{3,2,1,0:T(8,128)(2,1)S(1)} %stack.23), channel_id=1, replica_groups=mesh['tok'=16,'voc'=32] {'voc'}, dimensions={0} | all-to-all | bytes 294912 | tf_op jit(solution)/shard_map/all_to_all | solution.py:12
  29.3 0.1 copy.8
  29.4 1.0 reshape.43
  30.4 0.0 all-gather.2.cloned.1.call-update
  30.5 0.0 reduce-scatter.3.cloned.1.call-start
  30.5 43.2 %all-gather.2.cloned.1.call-done = bf16[2,256,2304]{2,1,0:T(8,128)(2,1)} async-done(((bf16[2,16,2304]{2,1,0:T(8,128)(2,1)}), bf16[2,256,2304]{2,1,0:T(8,128)(2,1)}) %all-gather.2.cloned.1.call-update) | async-done | bytes 2359312 | tf_op jit(solution)/shard_map/all_gather | solution.py:20
  73.7 2.4 fusion.3
  76.1 0.6 fusion.1
  76.8 1.3 fusion.9
  78.1 96.8 %psum.7 = f32[2,256]{1,0:T(2,128)S(1)} all-reduce(f32[2,256]{1,0:T(2,128)S(1)} %pad_maximum_fusion.1), channel_id=1, replica_groups=mesh['tok'=16,'voc'=32] {'tok','voc'}, use_global_device_ids=true, to_apply=%region_2.0 | all-reduce | flops 512 | bytes 4096 | tf_op jit(solution)/shard_map/psum | solution.py:31
  174.9 1.2 add_convert_fusion
  176.2 1.9 fusion.12
  178.1 2.0 convolution_add_fusion
  180.0 0.0 reduce-scatter.3.cloned.1.call-update
  180.1 0.0 all-reduce.3.cloned.1.call-start
  180.1 1.3 dynamic-slice
  182.0 57.4 %reduce-scatter.3.cloned.1.call-done = f32[16,2304]{1,0:T(8,128)} async-done(((f32[256,2304]{1,0:T(8,128)}), f32[16,2304]{1,0:T(8,128)}) %reduce-scatter.3.cloned.1.call-update) | async-done | bytes 147472 | tf_op jit(solution)/shard_map/reduce_scatter | solution.py:59
  239.4 0.0 all-reduce.3.cloned.1.call-update
  239.4 3.2 convolution_bitcast_fusion
  242.7 152.5 %all-reduce.3.cloned.1.call-done = f32[16,2304]{1,0:T(8,128)} async-done(((f32[16,2304]{1,0:T(8,128)}), f32[16,2304]{1,0:T(8,128)}) %all-reduce.3.cloned.1.call-update) | async-done | bytes 147472
  395.1 1.4 constant_dynamic-slice_fusion
  (16 shorter events, 0.1 us)
Async XLA Ops:
  7.2 69.0 %copy-start = (bf16[2304,256]{1,0:T(8,128)(2,1)S(1)}, bf16[2304,256]{1,0:T(8,128)(2,1)}, u32[]{:S(2)}) copy-start(bf16[2304,256]{1,0:T(8,128)(2,1)} %param.6) | copy-start | bytes 3538948
  7.2 66.6 %all-gather.2.cloned.1.call-start = ((), (), s32[]{:S(2)}) async-start(), calls=%async_computation.2 | async-start | bytes 2506752 | tf_op jit(solution)/shard_map/all_gather | solution.py:20
  30.5 209.0 %reduce-scatter.3.cloned.1.call-start = ((), (), s32[]{:S(2)}) async-start(), calls=%async_computation.3 | async-start | bytes 2506752 | tf_op jit(solution)/shard_map/reduce_scatter | solution.py:59
  73.7 2.4 copy-start.1
  76.7 1.3 copy-start.4
  76.8 98.1 %copy-start.5 = (s32[256]{0:T(256)S(1)}, s32[256]{0:T(256)}, u32[]{:S(2)}) copy-start(s32[256]{0:T(256)} %param.7) | copy-start | bytes 3076
  176.1 1.9 copy-start.3
  176.1 1.9 copy-start.2
  180.1 215.1 %all-reduce.3.cloned.1.call-start = ((), (), s32[]{:S(2)}) async-start(), calls=%async_computation.4 | async-start | bytes 294912
Sparse Core Ops, SparseCore 0:
  30.6 43.1 all-gather.1
  180.2 59.2 reduce-scatter.2
  242.9 152.2 all-reduce.2
